TPU v7x, 32 devices: a whole 2x2x4 slice. The times are simulated.
32 devices in a mesh: rep: 4 (over x, core), shard: 8 (over z, y).
Axes of the slice: x: 2, y: 2, z: 4, core: 2. Of those that a mesh axis runs over, the one named last changes fastest.
Arguments:
- tokens: bfloat16 [4096, 896], P(('rep', 'shard')), may hold values from -6 to 6
- cotangent: bfloat16 [4096, 896], P(('rep', 'shard')), may hold values from -6 to 6
- lengths: int32 [32, 8], P(('rep', 'shard')), may hold values from 1 to 64, 128 in all within a row
- query_weight: bfloat16 [896, 896], P('shard'), may hold values from -0.1875 to 0.1875
- key_weight: bfloat16 [896, 128], P('shard'), may hold values from -0.1875 to 0.1875
- value_weight: bfloat16 [896, 128], P('shard'), may hold values from -0.1875 to 0.1875
- output_weight: bfloat16 [896, 896], P('shard'), may hold values from -0.5 to 0.5
- query_bias: bfloat16 [896], P('shard'), may hold values from -3 to 3
- key_bias: bfloat16 [128], P('shard'), may hold values from -3 to 3
- value_bias: bfloat16 [128], P('shard'), may hold values from -3 to 3
- attn_gain: bfloat16 [896], P('shard'), may hold values from 0.5 to 1.5
- gate_weight: bfloat16 [896, 4864], P('shard'), may hold values from -0.1875 to 0.1875
- up_weight: bfloat16 [896, 4864], P('shard'), may hold values from -0.1875 to 0.1875
- down_weight: bfloat16 [4864, 896], P('shard'), may hold values from -0.15625 to 0.15625
- mlp_gain: bfloat16 [896], P('shard'), may hold values from 0.5 to 1.5
Outputs:
- result: bfloat16 [4096, 896], P(('rep', 'shard'))
- grad_tokens: float32 [4096, 896], P(('rep', 'shard'))
- grad_query_weight: float32 [896, 896], P('shard')
- grad_key_weight: float32 [896, 128], P('shard')
- grad_value_weight: float32 [896, 128], P('shard')
- grad_output_weight: float32 [896, 896], P('shard')
- grad_query_bias: float32 [896], P('shard')
- grad_key_bias: float32 [128], P('shard')
- grad_value_bias: float32 [128], P('shard')
- grad_attn_gain: float32 [896], P('shard')
- grad_gate_weight: float32 [896, 4864], P('shard')
- grad_up_weight: float32 [896, 4864], P('shard')
- grad_down_weight: float32 [4864, 896], P('shard')
- grad_mlp_gain: float32 [896], P('shard')
Inputs may be any that keep to these rules, and one draw needn't show every extreme that they name: Row b lists the lengths of the 8 sequences packed in order on the b-th block of 128 tokens; they fill it exactly, and the longest of every row is exactly 64.
All inputs are finite; a program needn't handle non-finite values.
Results may differ from a plain program's by a relative error of at most 0.02.
The roundings to bfloat16 on the way count: a program that leaves them out, or rounds other values in their place, can miss the bound.
Values may be sent and summed in bfloat16 or wider, within the bound.
A program may use at most 192 MiB of HBM per device.

v0:
```python
import math

import jax
import jax.numpy as jnp
from jax import lax
from jax.sharding import PartitionSpec as P

HEADS = 14
KVH = 2
HD = 64


theta_base = 1000000.0
eps_norm = 1e-06
masked_score = -1000000000.0


def times_transposed(left, weight):
    return lax.dot_general(
        left, weight, (((1,), (1,)), ((), ())), preferred_element_type=jnp.float32
    )


def tables(lengths_row, rows):
    ends = jnp.cumsum(lengths_row)
    starts = ends - lengths_row
    places = jnp.arange(rows, dtype=jnp.int32)
    inside = ((places[:, None] >= starts[None, :]) & (places[:, None] < ends[None, :])).astype(
        jnp.int32
    )
    slots = jnp.arange(lengths_row.shape[0], dtype=jnp.int32)
    segment = jnp.sum(inside * slots[None, :], axis=1)
    first = jnp.sum(inside * starts[None, :], axis=1)
    offset = (places - first).astype(jnp.float32)
    half = HD // 2
    freq = theta_base ** (-(jnp.arange(half, dtype=jnp.float32) * (2.0 / HD)))
    angles = offset[:, None] * freq[None, :]
    return (segment, places, jnp.cos(angles), jnp.sin(angles))


def rotate(values, cosine, sine):
    half = values.shape[-1] // 2
    first, second = (values[..., :half], values[..., half:])
    cosine = cosine[:, :, None, :]
    sine = sine[:, :, None, :]
    return jnp.concatenate(
        [first * cosine - second * sine, second * cosine + first * sine], axis=-1
    )


def unrotate(grads, cosine, sine):
    half = grads.shape[-1] // 2
    first, second = (grads[..., :half], grads[..., half:])
    cosine = cosine[:, :, None, :]
    sine = sine[:, :, None, :]
    return jnp.concatenate(
        [first * cosine + second * sine, second * cosine - first * sine], axis=-1
    )


def norm_fwd(hidden, gain):
    scale = lax.rsqrt(jnp.mean(hidden * hidden, axis=-1, keepdims=True) + eps_norm)
    return (scale, hidden * scale * gain.astype(jnp.float32))


def norm_bwd(dnormed, hidden, scale, gain):
    gain_f = gain.astype(jnp.float32)
    dgain = jnp.sum(dnormed * hidden * scale, axis=0)
    inner = dnormed * gain_f
    dhidden = scale * inner - hidden * (scale * scale * scale) * jnp.mean(
        inner * hidden, axis=-1, keepdims=True
    )
    return (dhidden, dgain)


def scores_of(query, keys, segment, places):
    raw = jnp.einsum("igha,jga->ghij", query, keys, preferred_element_type=jnp.float32) * (
        1.0 / math.sqrt(HD)
    )
    allowed = (segment[:, None] == segment[None, :]) & (places[None, :] <= places[:, None])
    return jnp.where(allowed[None, None], raw, masked_score)


def attend(query, keys, values, segment, places):
    raw = scores_of(query, keys, segment, places)
    top = jnp.max(raw, axis=-1, keepdims=True)
    total = jnp.sum(jnp.exp(raw - top), axis=-1)
    lse = top[..., 0] + jnp.log(total)
    probs = jnp.exp(raw - lse[..., None]).astype(jnp.bfloat16)
    mixed = jnp.einsum("ghij,jga->igha", probs, values, preferred_element_type=jnp.float32).astype(
        jnp.bfloat16
    )
    return (mixed, lse)


def attend_back(query, keys, values, mixed, dmixed, lse, segment, places):
    raw = scores_of(query, keys, segment, places)
    probs_f = jnp.exp(raw - lse[..., None])
    probs = probs_f.astype(jnp.bfloat16)
    dvals = jnp.einsum("ghij,igha->jga", probs, dmixed, preferred_element_type=jnp.float32)
    dprobs = jnp.einsum("igha,jga->ghij", dmixed, values, preferred_element_type=jnp.float32)
    delta = jnp.einsum("igha,igha->ghi", dmixed, mixed, preferred_element_type=jnp.float32)
    dscores = (probs_f * (dprobs - delta[..., None]) * (1.0 / math.sqrt(HD))).astype(jnp.bfloat16)
    dquery = jnp.einsum("ghij,jga->igha", dscores, keys, preferred_element_type=jnp.float32)
    dkeys = jnp.einsum("ghij,igha->jga", dscores, query, preferred_element_type=jnp.float32)
    return (dquery, dkeys, dvals)


def forward(tokens, lengths, attn_params, mlp_params):
    blocks, rows, width = tokens.shape
    (
        query_weight,
        key_weight,
        value_weight,
        output_weight,
        query_bias,
        key_bias,
        value_bias,
        attn_gain,
    ) = attn_params
    gate_weight, up_weight, down_weight, mlp_gain = mlp_params
    segment, places, cosine, sine = jax.vmap(lambda lens: tables(lens, rows))(lengths)
    flat = tokens.reshape(blocks * rows, width).astype(jnp.float32)
    scale_one, normed_one = norm_fwd(flat, attn_gain)
    normed_one = normed_one.astype(jnp.bfloat16)
    query = jnp.dot(
        normed_one, query_weight, preferred_element_type=jnp.float32
    ) + query_bias.astype(jnp.float32)
    keys = jnp.dot(normed_one, key_weight, preferred_element_type=jnp.float32) + key_bias.astype(
        jnp.float32
    )
    values = jnp.dot(
        normed_one, value_weight, preferred_element_type=jnp.float32
    ) + value_bias.astype(jnp.float32)
    query = rotate(query.reshape(blocks, rows, HEADS, HD), cosine, sine).astype(jnp.bfloat16)
    query = query.reshape(blocks, rows, KVH, HEADS // KVH, HD)
    keys = rotate(keys.reshape(blocks, rows, KVH, HD), cosine, sine).astype(jnp.bfloat16)
    values = values.reshape(blocks, rows, KVH, HD).astype(jnp.bfloat16)
    mixed, lse = jax.vmap(attend)(query, keys, values, segment, places)
    mixed_flat = mixed.reshape(blocks * rows, width)
    hidden_one = flat + jnp.dot(mixed_flat, output_weight, preferred_element_type=jnp.float32)
    scale_two, normed_two = norm_fwd(hidden_one, mlp_gain)
    normed_two = normed_two.astype(jnp.bfloat16)
    gate = jnp.dot(normed_two, gate_weight, preferred_element_type=jnp.float32)
    upper = jnp.dot(normed_two, up_weight, preferred_element_type=jnp.float32)
    product = (jax.nn.silu(gate) * upper).astype(jnp.bfloat16)
    result = (
        hidden_one + jnp.dot(product, down_weight, preferred_element_type=jnp.float32)
    ).astype(jnp.bfloat16)
    saved = (
        segment,
        places,
        cosine,
        sine,
        flat,
        scale_one,
        normed_one,
        query,
        keys,
        values,
        mixed,
        lse,
        hidden_one,
        scale_two,
        normed_two,
        gate,
        upper,
        product,
    )
    return (result, saved)


def backward(cotangent, saved, attn_params, mlp_params):
    blocks, rows, width = cotangent.shape
    (
        query_weight,
        key_weight,
        value_weight,
        output_weight,
        query_bias,
        key_bias,
        value_bias,
        attn_gain,
    ) = attn_params
    gate_weight, up_weight, down_weight, mlp_gain = mlp_params
    (
        segment,
        places,
        cosine,
        sine,
        flat,
        scale_one,
        normed_one,
        query,
        keys,
        values,
        mixed,
        lse,
        hidden_one,
        scale_two,
        normed_two,
        gate,
        upper,
        product,
    ) = saved
    cot_b = cotangent.reshape(blocks * rows, width)
    cot_f = cot_b.astype(jnp.float32)
    grad_down = jnp.dot(product.T, cot_b, preferred_element_type=jnp.float32)
    dprod = times_transposed(cot_b, down_weight)
    sigma = jax.nn.sigmoid(gate)
    dgate = (dprod * upper * sigma * (1.0 + gate * (1.0 - sigma))).astype(jnp.bfloat16)
    dup = (dprod * gate * sigma).astype(jnp.bfloat16)
    grad_gate = jnp.dot(normed_two.T, dgate, preferred_element_type=jnp.float32)
    grad_up = jnp.dot(normed_two.T, dup, preferred_element_type=jnp.float32)
    dnormed_two = times_transposed(dgate, gate_weight) + times_transposed(dup, up_weight)
    dh_two, grad_mlp_gain = norm_bwd(dnormed_two, hidden_one, scale_two, mlp_gain)
    dhidden = cot_f + dh_two
    dres = dhidden.astype(jnp.bfloat16)
    mixed_flat = mixed.reshape(blocks * rows, width)
    grad_output = jnp.dot(mixed_flat.T, dres, preferred_element_type=jnp.float32)
    dmixed = times_transposed(dres, output_weight).astype(jnp.bfloat16)
    dmixed = dmixed.reshape(blocks, rows, KVH, HEADS // KVH, HD)
    dquery, dkeys, dvals = jax.vmap(attend_back)(
        query, keys, values, mixed, dmixed, lse, segment, places
    )
    dquery = unrotate(dquery.reshape(blocks, rows, HEADS, HD), cosine, sine).reshape(
        blocks * rows, width
    )
    dkeys = unrotate(dkeys, cosine, sine).reshape(blocks * rows, KVH * HD)
    dvals = dvals.reshape(blocks * rows, KVH * HD)
    grad_qbias = jnp.sum(dquery, axis=0)
    grad_kbias = jnp.sum(dkeys, axis=0)
    grad_vbias = jnp.sum(dvals, axis=0)
    dquery_b = dquery.astype(jnp.bfloat16)
    dkeys_b = dkeys.astype(jnp.bfloat16)
    dvals_b = dvals.astype(jnp.bfloat16)
    grad_query = jnp.dot(normed_one.T, dquery_b, preferred_element_type=jnp.float32)
    grad_key = jnp.dot(normed_one.T, dkeys_b, preferred_element_type=jnp.float32)
    grad_value = jnp.dot(normed_one.T, dvals_b, preferred_element_type=jnp.float32)
    dnormed_one = (
        times_transposed(dquery_b, query_weight)
        + times_transposed(dkeys_b, key_weight)
        + times_transposed(dvals_b, value_weight)
    )
    dh_one, grad_attn_gain = norm_bwd(dnormed_one, flat, scale_one, attn_gain)
    grad_input = dhidden + dh_one
    attn_grads = (
        grad_query,
        grad_key,
        grad_value,
        grad_output,
        grad_qbias,
        grad_kbias,
        grad_vbias,
        grad_attn_gain,
    )
    mlp_grads = (grad_gate, grad_up, grad_down, grad_mlp_gain)
    return (grad_input, attn_grads, mlp_grads)


def on_device(
    tokens,
    cotangent,
    lengths,
    query_weight,
    key_weight,
    value_weight,
    output_weight,
    query_bias,
    key_bias,
    value_bias,
    attn_gain,
    gate_weight,
    up_weight,
    down_weight,
    mlp_gain,
):
    attn_params = (
        lax.all_gather(query_weight, "shard", axis=0, tiled=True),
        lax.all_gather(key_weight, "shard", axis=0, tiled=True),
        lax.all_gather(value_weight, "shard", axis=0, tiled=True),
        lax.all_gather(output_weight, "shard", axis=0, tiled=True),
        lax.all_gather(query_bias, "shard", axis=0, tiled=True),
        lax.all_gather(key_bias, "shard", axis=0, tiled=True),
        lax.all_gather(value_bias, "shard", axis=0, tiled=True),
        lax.all_gather(attn_gain, "shard", axis=0, tiled=True),
    )
    mlp_params = (
        lax.all_gather(gate_weight, "shard", axis=0, tiled=True),
        lax.all_gather(up_weight, "shard", axis=0, tiled=True),
        lax.all_gather(down_weight, "shard", axis=0, tiled=True),
        lax.all_gather(mlp_gain, "shard", axis=0, tiled=True),
    )
    result, saved = forward(tokens[None], lengths, attn_params, mlp_params)
    attn_back, mlp_back = (attn_params, mlp_params)
    grad_input, attn_grads, mlp_grads = backward(cotangent[None], saved, attn_back, mlp_back)
    grad_gate, grad_up, grad_down, grad_mlp_gain = mlp_grads
    (
        grad_query,
        grad_key,
        grad_value,
        grad_output,
        grad_qbias,
        grad_kbias,
        grad_vbias,
        grad_attn_gain,
    ) = attn_grads
    down_owned = lax.psum_scatter(
        grad_down.astype(jnp.bfloat16), "shard", scatter_dimension=0, tiled=True
    )
    gate_owned, up_owned, mlp_gain_owned = (
        lax.psum_scatter(
            grad_gate.astype(jnp.bfloat16), "shard", scatter_dimension=0, tiled=True
        ).astype(jnp.float32),
        lax.psum_scatter(
            grad_up.astype(jnp.bfloat16), "shard", scatter_dimension=0, tiled=True
        ).astype(jnp.float32),
        lax.psum_scatter(
            grad_mlp_gain.astype(jnp.bfloat16), "shard", scatter_dimension=0, tiled=True
        ).astype(jnp.float32),
    )
    owned = (
        lax.psum_scatter(grad_query, "shard", scatter_dimension=0, tiled=True),
        lax.psum_scatter(grad_key, "shard", scatter_dimension=0, tiled=True),
        lax.psum_scatter(grad_value, "shard", scatter_dimension=0, tiled=True),
        lax.psum_scatter(grad_output, "shard", scatter_dimension=0, tiled=True),
        lax.psum_scatter(grad_qbias, "shard", scatter_dimension=0, tiled=True),
        lax.psum_scatter(grad_kbias, "shard", scatter_dimension=0, tiled=True),
        lax.psum_scatter(grad_vbias, "shard", scatter_dimension=0, tiled=True),
        lax.psum_scatter(grad_attn_gain, "shard", scatter_dimension=0, tiled=True),
    )
    split = (
        lax.psum_scatter(
            owned[0].astype(jnp.bfloat16), "rep", scatter_dimension=1, tiled=True
        ).astype(jnp.float32),
        lax.psum_scatter(
            owned[1].astype(jnp.bfloat16), "rep", scatter_dimension=1, tiled=True
        ).astype(jnp.float32),
        lax.psum_scatter(
            owned[2].astype(jnp.bfloat16), "rep", scatter_dimension=1, tiled=True
        ).astype(jnp.float32),
        lax.psum_scatter(
            owned[3].astype(jnp.bfloat16), "rep", scatter_dimension=1, tiled=True
        ).astype(jnp.float32),
        lax.psum_scatter(
            gate_owned.astype(jnp.bfloat16), "rep", scatter_dimension=1, tiled=True
        ).astype(jnp.float32),
        lax.psum_scatter(
            up_owned.astype(jnp.bfloat16), "rep", scatter_dimension=1, tiled=True
        ).astype(jnp.float32),
        lax.psum_scatter(down_owned, "rep", scatter_dimension=1, tiled=True).astype(jnp.float32),
    )
    small_tot = lax.psum((owned[4], owned[5], owned[6], owned[7], mlp_gain_owned), "rep")
    mats = (
        lax.all_gather(split[0].astype(jnp.bfloat16), "rep", axis=1, tiled=True).astype(
            jnp.float32
        ),
        lax.all_gather(split[1].astype(jnp.bfloat16), "rep", axis=1, tiled=True).astype(
            jnp.float32
        ),
        lax.all_gather(split[2].astype(jnp.bfloat16), "rep", axis=1, tiled=True).astype(
            jnp.float32
        ),
        lax.all_gather(split[3].astype(jnp.bfloat16), "rep", axis=1, tiled=True).astype(
            jnp.float32
        ),
        lax.all_gather(split[4].astype(jnp.bfloat16), "rep", axis=1, tiled=True).astype(
            jnp.float32
        ),
        lax.all_gather(split[5].astype(jnp.bfloat16), "rep", axis=1, tiled=True).astype(
            jnp.float32
        ),
        lax.all_gather(split[6].astype(jnp.bfloat16), "rep", axis=1, tiled=True).astype(
            jnp.float32
        ),
    )
    return (
        result,
        grad_input,
        mats[0],
        mats[1],
        mats[2],
        mats[3],
        small_tot[0],
        small_tot[1],
        small_tot[2],
        small_tot[3],
        mats[4],
        mats[5],
        mats[6],
        small_tot[4],
    )


def solution(mesh):
    in_specs = (
        P(("rep", "shard"), None),
        P(("rep", "shard"), None),
        P(("rep", "shard"), None),
        P("shard", None),
        P("shard", None),
        P("shard", None),
        P("shard", None),
        P("shard"),
        P("shard"),
        P("shard"),
        P("shard"),
        P("shard", None),
        P("shard", None),
        P("shard", None),
        P("shard"),
    )
    out_specs = (
        P(("rep", "shard"), None),
        P(("rep", "shard"), None),
        P("shard", None),
        P("shard", None),
        P("shard", None),
        P("shard", None),
        P("shard"),
        P("shard"),
        P("shard"),
        P("shard"),
        P("shard", None),
        P("shard", None),
        P("shard", None),
        P("shard"),
    )
    return jax.shard_map(
        on_device, mesh=mesh, in_specs=in_specs, out_specs=out_specs, check_vma=False
    )
```

profile of v0, /device:TPU:0, one launch (start us, length us, event | category | flops | bytes accessed | tf_op | source)
XLA Modules:
  0.0 1498.0 jit_solution(12919603139877191212)
XLA Ops:
  13.8 23.7 %all-reduce.12 = (bf16[128]{0:T(256)(128)(2,1)S(1)}, bf16[896]{0:T(1024)(128)(2,1)S(1)}, bf16[896]{0:T(1024)(128)(2,1)S(1)}, bf16[128]{0:T(256)(128)(2,1)S(1)}, bf16[896]{0:T(1024)(128)(2,1)S(1)}) all-reduce(bf16[128]{0:T(256)(128)(2,1)S(1)} %dynamic-update-slice.1, ...), channel_id=1, replica_groups=mesh['rep'=4,'shard'=8] {'shard'}, use_global_device_ids=true, to_apply=%add.1 | all-reduce | flops 2944 | bytes 11776
  37.8 31.2 %all_gather.58 = bf16[896,128]{1,0:T(8,128)(2,1)S(1)} all-gather(bf16[112,128]{1,0:T(8,128)(2,1)S(1)} %copy-done.29), channel_id=1, replica_groups=mesh['rep'=4,'shard'=8] {'shard'}, dimensions={0}, use_global_device_ids=true | all-gather | bytes 258048 | tf_op jit(solution)/shard_map/all_gather | solution.py:281
  69.0 31.2 %all_gather.60 = bf16[896,128]{1,0:T(8,128)(2,1)S(1)} all-gather(bf16[112,128]{1,0:T(8,128)(2,1)S(1)} %copy-done.30), channel_id=1, replica_groups=mesh['rep'=4,'shard'=8] {'shard'}, dimensions={0}, use_global_device_ids=true | all-gather | bytes 258048 | tf_op jit(solution)/shard_map/all_gather | solution.py:280
  101.9 1.9 convolution_add_fusion.3
  106.4 2.0 multiply_reduce_fusion.2
  109.0 126.7 %all-gather.15.cloned.1.call-done = bf16[896,4864]{1,0:T(8,128)(2,1)} async-done(((bf16[112,4864]{1,0:T(8,128)(2,1)}), bf16[896,4864]{1,0:T(8,128)(2,1)}) %all-gather.15.cloned.1.call-update) | async-done | bytes 8716304 | tf_op jit(solution)/shard_map/all_gather | solution.py:289
  235.8 6.4 fusion.50
  242.1 122.3 %all-gather.17.cloned.1.call-done = bf16[896,4864]{1,0:T(8,128)(2,1)} async-done(((bf16[112,4864]{1,0:T(8,128)(2,1)}), bf16[896,4864]{1,0:T(8,128)(2,1)}) %all-gather.17.cloned.1.call-update) | async-done | bytes 8716304 | tf_op jit(solution)/shard_map/all_gather | solution.py:290
  364.5 6.5 fusion.51
  371.0 122.2 %all-gather.19.cloned.1.call-done = bf16[4864,896]{1,0:T(8,128)(2,1)} async-done(((bf16[608,896]{1,0:T(8,128)(2,1)}), bf16[4864,896]{1,0:T(8,128)(2,1)}) %all-gather.19.cloned.1.call-update) | async-done | bytes 8716304 | tf_op jit(solution)/shard_map/all_gather | solution.py:291
  493.2 8.5 multiply_convert_fusion
  502.7 5.8 convolution_convert_fusion.2
  508.8 7.4 convolution_convert_fusion.1
  516.3 4.7 convolution_convert_fusion
  521.1 6.8 fusion.52
  528.0 7.1 multiply_reduce_fusion
  550.7 2.3 fusion.42
  553.9 2.3 fusion.25
  556.3 103.2 %reduce-scatter.37.cloned.1.call-done = bf16[112,4864]{1,0:T(8,128)(2,1)} async-done(((bf16[896,4864]{1,0:T(8,128)(2,1)}), bf16[112,4864]{1,0:T(8,128)(2,1)}) %reduce-scatter.37.cloned.1.call-update) | async-done | bytes 1089552 | tf_op jit(solution)/shard_map/reduce_scatter | solution.py:312
  659.5 2.4 copy.109
  661.9 152.9 %reduce-scatter.39.cloned.1.call-done = bf16[112,4864]{1,0:T(8,128)(2,1)} async-done(((bf16[896,4864]{1,0:T(8,128)(2,1)}), bf16[112,4864]{1,0:T(8,128)(2,1)}) %reduce-scatter.39.cloned.1.call-update) | async-done | bytes 1089552 | tf_op jit(solution)/shard_map/reduce_scatter | solution.py:315
  814.8 2.4 copy.111
  817.2 152.9 %reduce-scatter.41.cloned.1.call-done = bf16[608,896]{1,0:T(8,128)(2,1)} async-done(((bf16[4864,896]{1,0:T(8,128)(2,1)}), bf16[608,896]{1,0:T(8,128)(2,1)}) %reduce-scatter.41.cloned.1.call-update) | async-done | bytes 1089552 | tf_op jit(solution)/shard_map/reduce_scatter | solution.py:308
  970.1 2.4 copy.113
  972.6 62.5 %reduce-scatter.31.cloned.1.call-done = f32[112,128]{1,0:T(8,128)} async-done(((f32[896,128]{1,0:T(8,128)}), f32[112,128]{1,0:T(8,128)}) %reduce-scatter.31.cloned.1.call-update) | async-done | bytes 57360 | tf_op jit(solution)/shard_map/reduce_scatter | solution.py:324
  1036.7 63.1 %reduce-scatter.33.cloned.1.call-done = f32[112,128]{1,0:T(8,128)} async-done(((f32[896,128]{1,0:T(8,128)}), f32[112,128]{1,0:T(8,128)}) %reduce-scatter.33.cloned.1.call-update) | async-done | bytes 57360 | tf_op jit(solution)/shard_map/reduce_scatter | solution.py:325
  1101.3 76.8 %reduce-scatter.29.cloned.1.call-done = f32[112,896]{1,0:T(8,128)} async-done(((f32[896,896]{1,0:T(8,128)}), f32[112,896]{1,0:T(8,128)}) %reduce-scatter.29.cloned.1.call-update) | async-done | bytes 401424 | tf_op jit(solution)/shard_map/reduce_scatter | solution.py:323
  1180.1 76.3 %reduce-scatter.35.cloned.1.call-done = f32[112,896]{1,0:T(8,128)} async-done(((f32[896,896]{1,0:T(8,128)}), f32[112,896]{1,0:T(8,128)}) %reduce-scatter.35.cloned.1.call-update) | async-done | bytes 401424 | tf_op jit(solution)/shard_map/reduce_scatter | solution.py:326
  1258.3 26.3 %reduce-scatter.51.cloned.1.call-done = bf16[1216,112]{1,0:T(8,128)(2,1)} async-done(((bf16[4864,112]{1,0:T(8,128)(2,1)}), bf16[1216,112]{1,0:T(8,128)(2,1)}) %reduce-scatter.51.cloned.1.call-update) | async-done | bytes 272400
  1286.7 26.9 %reduce-scatter.53.cloned.1.call-done = bf16[1216,112]{1,0:T(8,128)(2,1)} async-done(((bf16[4864,112]{1,0:T(8,128)(2,1)}), bf16[1216,112]{1,0:T(8,128)(2,1)}) %reduce-scatter.53.cloned.1.call-update) | async-done | bytes 272400
  1313.6 1.9 copy.112
  1319.2 2.0 fusion.53
  1322.5 19.6 %reduce-scatter.55.cloned.1.call-done = bf16[224,608]{1,0:T(8,128)(2,1)} async-done(((bf16[896,608]{1,0:T(8,128)(2,1)}), bf16[224,608]{1,0:T(8,128)(2,1)}) %reduce-scatter.55.cloned.1.call-update) | async-done | bytes 272400
  1343.8 22.0 %all-reduce.10 = (f32[896]{0:T(1024)S(1)}, f32[128]{0:T(128)S(1)}, f32[128]{0:T(128)S(1)}, f32[896]{0:T(1024)S(1)}) all-reduce(f32[896]{0:T(1024)S(1)} %reduce_sum.122, f32[128]{0:T(128)} %reduce_sum.124, f32[128]{0:T(128)} %reduce_sum.126, f32[896]{0:T(1024)S(1)} %get-tuple-element.44), channel_id=10, replica_groups=mesh['rep'=4,'shard'=8] {'shard'}, use_global_device_ids=true, to_apply=%region_18.19.clone | all-reduce | flops 2048 | bytes 16384
  1366.1 17.3 %all-reduce.9 = bf16[896]{0:T(1024)(128)(2,1)S(1)} all-reduce(bf16[896]{0:T(1024)(128)(2,1)} %get-tuple-element.42), channel_id=20, replica_groups=mesh['rep'=4,'shard'=8] {'shard'}, use_global_device_ids=true, to_apply=%region_36.37.clone | all-reduce | flops 896 | bytes 3584
  1383.4 6.5 all-reduce.11
  1392.1 5.7 fusion.7
  1397.8 5.3 all_gather.70
  1403.9 5.4 all_gather.71
  1410.0 5.9 all_gather.69
  1416.8 14.2 reduce-scatter.49.cloned.1.call-done
  1430.9 5.9 all_gather.72
  1437.7 12.5 all-gather.23.cloned.1.call-done
  1452.0 2.7 reshape.560
  1454.7 14.9 all-gather.25.cloned.1.call-done
  1471.5 2.7 reshape.561
  1474.1 14.3 all-gather.21.cloned.1.call-done
  1488.5 2.7 copy.84
  (221 shorter events, 52.1 us)
Async XLA Ops:
  7.2 5.4 copy-start.40
  7.2 5.7 copy-start.41
  7.2 5.9 copy-start.42
  7.2 6.1 copy-start.43
  7.2 6.4 copy-start.44
  7.2 30.3 %copy-start.45 = (s32[1,8]{1,0:T(1,128)S(1)}, s32[1,8]{1,0:T(1,128)}, u32[]{:S(2)}) copy-start(s32[1,8]{1,0:T(1,128)} %param.17) | copy-start | bytes 100
  7.3 30.5 %copy-start.29 = (bf16[112,128]{1,0:T(8,128)(2,1)S(1)}, bf16[112,128]{1,0:T(8,128)(2,1)}, u32[]{:S(2)}) copy-start(bf16[112,128]{1,0:T(8,128)(2,1)} %param.20) | copy-start | bytes 86020
  7.3 61.7 %copy-start.30 = (bf16[112,128]{1,0:T(8,128)(2,1)S(1)}, bf16[112,128]{1,0:T(8,128)(2,1)}, u32[]{:S(2)}) copy-start(bf16[112,128]{1,0:T(8,128)(2,1)} %param.19) | copy-start | bytes 86020
  7.3 93.0 %copy-start = (bf16[128,896]{1,0:T(8,128)(2,1)S(1)}, bf16[128,896]{1,0:T(8,128)(2,1)}, u32[]{:S(2)}) copy-start(bf16[128,896]{1,0:T(8,128)(2,1)} %param.15) | copy-start | bytes 688132
  7.3 94.6 %all-gather.11.cloned.1.call-start = ((), (), s32[]{:S(2)}) async-start(), calls=%async_computation.14 | async-start | bytes 1806336 | tf_op jit(solution)/shard_map/all_gather | solution.py:279
  8.0 98.4 %all-gather.13.cloned.1.call-start = ((), (), s32[]{:S(2)}) async-start(), calls=%async_computation.15 | async-start | bytes 1806336 | tf_op jit(solution)/shard_map/all_gather | solution.py:282
  8.8 227.0 %all-gather.15.cloned.1.call-start = ((), (), s32[]{:S(2)}) async-start(), calls=%async_computation.16 | async-start | bytes 9805824 | tf_op jit(solution)/shard_map/all_gather | solution.py:289
  9.5 355.0 %all-gather.17.cloned.1.call-start = ((), (), s32[]{:S(2)}) async-start(), calls=%async_computation.17 | async-start | bytes 9805824 | tf_op jit(solution)/shard_map/all_gather | solution.py:290
  10.1 483.1 %all-gather.19.cloned.1.call-start = ((), (), s32[]{:S(2)}) async-start(), calls=%async_computation.18 | async-start | bytes 9805824 | tf_op jit(solution)/shard_map/all_gather | solution.py:291
  10.7 648.8 %reduce-scatter.37.cloned.1.call-start = ((), (), s32[]{:S(2)}) async-start(), calls=%async_computation.23 | async-start | bytes 9805824 | tf_op jit(solution)/shard_map/reduce_scatter | solution.py:312
  37.5 66.5 %copy-start.19 = (f32[896]{0:T(1024)}, f32[896]{0:T(1024)S(1)}, u32[]{:S(2)}) copy-start(f32[896]{0:T(1024)S(1)} %convert_element_type.179) | copy-start | bytes 10756
  37.6 71.3 %copy-start.27 = (f32[896]{0:T(1024)}, f32[896]{0:T(1024)S(1)}, u32[]{:S(2)}) copy-start(f32[896]{0:T(1024)S(1)} %convert_element_type.191) | copy-start | bytes 10756
  69.0 32.9 %copy-start.8 = (bf16[896,128]{1,0:T(8,128)(2,1)}, bf16[896,128]{1,0:T(8,128)(2,1)S(1)}, u32[]{:S(2)}) copy-start(bf16[896,128]{1,0:T(8,128)(2,1)S(1)} %all_gather.58) | copy-start | bytes 688132
  105.0 137.1 %copy-start.5 = (bf16[2,64,7,128]{3,1,2,0:T(8,128)(2,1)}, bf16[2,64,7,128]{3,1,2,0:T(8,128)(2,1)S(1)}, u32[]{:S(2)}) copy-start(bf16[2,64,7,128]{3,1,2,0:T(8,128)(2,1)S(1)} %convolution_convert_fusion.4) | copy-start | bytes 688132
  108.9 126.9 %copy-start.35 = (f32[128]{0:T(128)}, f32[128]{0:T(128)S(1)}, u32[]{:S(2)}) copy-start(f32[128]{0:T(128)S(1)} %get-tuple-element.82) | copy-start | bytes 1540
  242.1 251.0 %copy-start.7 = (bf16[128,896]{1,0:T(8,128)(2,1)S(1)}, bf16[128,896]{1,0:T(8,128)(2,1)}, u32[]{:S(2)}) copy-start(bf16[128,896]{1,0:T(8,128)(2,1)} %param.16) | copy-start | bytes 688132
  508.5 306.3 %reduce-scatter.39.cloned.1.call-start = ((), (), s32[]{:S(2)}) async-start(), calls=%async_computation.24 | async-start | bytes 9805824 | tf_op jit(solution)/shard_map/reduce_scatter | solution.py:315
  516.2 453.9 %reduce-scatter.41.cloned.1.call-start = ((), (), s32[]{:S(2)}) async-start(), calls=%async_computation.25 | async-start | bytes 9805824 | tf_op jit(solution)/shard_map/reduce_scatter | solution.py:308
  521.0 514.0 %reduce-scatter.31.cloned.1.call-start = ((), (), s32[]{:S(2)}) async-start(), calls=%async_computation.20 | async-start | bytes 516096 | tf_op jit(solution)/shard_map/reduce_scatter | solution.py:324
  521.1 6.8 copy-start.2
  521.1 6.8 copy-start.28
  521.1 6.8 copy-start.36
  527.9 7.1 copy-start.39
  528.0 7.3 copy-start.1
  537.7 5.5 copy-start.20
  537.7 5.5 copy-start.32
  544.3 555.4 %reduce-scatter.33.cloned.1.call-start = ((), (), s32[]{:S(2)}) async-start(), calls=%async_computation.21 | async-start | bytes 516096 | tf_op jit(solution)/shard_map/reduce_scatter | solution.py:325
  548.5 629.7 %reduce-scatter.29.cloned.1.call-start = ((), (), s32[]{:S(2)}) async-start(), calls=%async_computation.19 | async-start | bytes 3612672 | tf_op jit(solution)/shard_map/reduce_scatter | solution.py:323
  553.0 703.3 %reduce-scatter.35.cloned.1.call-start = ((), (), s32[]{:S(2)}) async-start(), calls=%async_computation.22 | async-start | bytes 3612672 | tf_op jit(solution)/shard_map/reduce_scatter | solution.py:326
  556.2 728.3 %reduce-scatter.51.cloned.1.call-start = ((), (), s32[]{:S(2)}) async-start(), calls=%async_computation.33 | async-start | bytes 1556480
  661.9 651.8 %reduce-scatter.53.cloned.1.call-start = ((), (), s32[]{:S(2)}) async-start(), calls=%async_computation.34 | async-start | bytes 1556480
  817.2 524.9 %reduce-scatter.55.cloned.1.call-start = ((), (), s32[]{:S(2)}) async-start(), calls=%async_computation.35 | async-start | bytes 1433600
  972.5 425.3 %reduce-scatter.45.cloned.1.call-start = ((), (), s32[]{:S(2)}) async-start(), calls=%async_computation.30 | async-start | bytes 40960
  1036.6 367.3 %reduce-scatter.47.cloned.1.call-start = ((), (), s32[]{:S(2)}) async-start(), calls=%async_computation.31 | async-start | bytes 40960
  1100.6 218.1 %copy-start.38 = (f32[2,64]{1,0:T(2,128)S(1)}, f32[2,64]{1,0:T(2,128)}, u32[]{:S(2)}) copy-start(f32[2,64]{1,0:T(2,128)} %get-tuple-element.73) | copy-start | bytes 1540
  1101.3 308.7 %reduce-scatter.43.cloned.1.call-start = ((), (), s32[]{:S(2)}) async-start(), calls=%async_computation.29 | async-start | bytes 286720
  1180.0 250.9 %reduce-scatter.49.cloned.1.call-start = ((), (), s32[]{:S(2)}) async-start(), calls=%async_computation.32 | async-start | bytes 286720
  1258.2 191.9 %all-gather.23.cloned.1.call-start = ((), (), s32[]{:S(2)}) async-start(), calls=%async_computation.27 | async-start | bytes 1433600 | tf_op jit(solution)/shard_map/all_gather | solution.py:367
  1286.4 183.2 %all-gather.25.cloned.1.call-start = ((), (), s32[]{:S(2)}) async-start(), calls=%async_computation.28 | async-start | bytes 1433600 | tf_op jit(solution)/shard_map/all_gather | solution.py:370
  1313.6 28.5 %copy-start.9 = (bf16[896,128]{1,0:T(8,128)(2,1)S(1)}, bf16[896,128]{1,0:T(8,128)(2,1)}, u32[]{:S(2)}) copy-start(bf16[896,128]{1,0:T(8,128)(2,1)} %copy-done.8) | copy-start | bytes 688132
  1313.6 28.5 %copy-start.22 = (f32[896]{0:T(1024)S(1)}, f32[896]{0:T(1024)}, u32[]{:S(2)}) copy-start(f32[896]{0:T(1024)} %copy-done.19) | copy-start | bytes 10756
  1313.6 28.5 %copy-start.34 = (f32[128]{0:T(128)S(1)}, f32[128]{0:T(128)}, u32[]{:S(2)}) copy-start(f32[128]{0:T(128)} %copy-done.31) | copy-start | bytes 1540
  1315.5 172.9 %all-gather.21.cloned.1.call-start = ((), (), s32[]{:S(2)}) async-start(), calls=%async_computation.26 | async-start | bytes 1433600 | tf_op jit(solution)/shard_map/all_gather | solution.py:373
  (20 other events, 45.1 us)
Sparse Core Ops, SparseCore 0:
  10.3 49.0 all-gather.10
  61.6 44.7 all-gather.12
  108.6 127.1 all-gather.14
  237.8 126.6 all-gather.16
  366.5 126.6 all-gather.18
  508.7 150.7 reduce-scatter.36
  663.1 151.6 reduce-scatter.38
  818.4 151.6 reduce-scatter.40
  973.4 61.5 reduce-scatter.30
  1038.2 61.5 reduce-scatter.32
  1103.3 74.7 reduce-scatter.28
  1181.6 74.6 reduce-scatter.34
  1259.5 24.9 reduce-scatter.50
  1287.6 26.0 reduce-scatter.52
  1316.6 25.4 reduce-scatter.54
  1344.3 19.5 reduce-scatter.44
  1366.1 19.5 reduce-scatter.46
  1388.6 19.9 reduce-scatter.42
  1411.0 19.8 reduce-scatter.48
  1432.9 17.2 all-gather.22
  1452.3 17.2 all-gather.24
  1471.2 17.2 all-gather.20
where the time goes:
time: 1500 us
  waiting for transfers between devices  1190 us (79%)
  blocking collectives  154 us (10%)
  matrix products  83.1 us (6%)
  local copies, waits for them, and re-layouts  38.2 us (3%)
  between operations  17.7 us (1%)
    reduce_scatter x1, waiting for transfers between devices, on_device(): lax.psum_scatter(grad_up.astype(jnp.bfloat16), 'shard', scatter_dimension...  153 us
    reduce_scatter x1, waiting for transfers between devices, on_device(): lax.psum_scatter(grad_down.astype(jnp.bfloat16), 'shard', scatter_dimensi...  153 us
    all_gather x1, waiting for transfers between devices, on_device(): lax.all_gather(gate_weight, 'shard', axis=0, tiled=True)  127 us
    all_gather x1, waiting for transfers between devices, on_device(): lax.all_gather(up_weight, 'shard', axis=0, tiled=True)  122 us
    all_gather x1, waiting for transfers between devices, on_device(): lax.all_gather(down_weight, 'shard', axis=0, tiled=True)  122 us
    reduce_scatter x1, waiting for transfers between devices, on_device(): lax.psum_scatter(grad_gate.astype(jnp.bfloat16), 'shard', scatter_dimensi...  103 us
    unnamed x29, waiting for transfers between devices  90.3 us
    reduce_scatter x1, waiting for transfers between devices, on_device(): lax.psum_scatter(grad_query, 'shard', scatter_dimension=0, tiled=True)  76.8 us
  transfers between devices with their start and end apart: 22, of which 18 were waited for; matrix products, arithmetic and copies ran while one was open for 7% of the time, Pallas kernels for 0%

commit v1 on v0

v1 whole, which is shorter than its diff:
```python
import math

import jax
import jax.numpy as jnp
from jax import lax
from jax.sharding import PartitionSpec as P

HEADS = 14
KVH = 2
HD = 64


theta_base = 1000000.0
eps_norm = 1e-06
masked_score = -1000000000.0


def times_transposed(left, weight):
    return lax.dot_general(
        left, weight, (((1,), (1,)), ((), ())), preferred_element_type=jnp.float32
    )


def tables(lengths_row, rows):
    ends = jnp.cumsum(lengths_row)
    starts = ends - lengths_row
    places = jnp.arange(rows, dtype=jnp.int32)
    inside = ((places[:, None] >= starts[None, :]) & (places[:, None] < ends[None, :])).astype(
        jnp.int32
    )
    slots = jnp.arange(lengths_row.shape[0], dtype=jnp.int32)
    segment = jnp.sum(inside * slots[None, :], axis=1)
    first = jnp.sum(inside * starts[None, :], axis=1)
    offset = (places - first).astype(jnp.float32)
    half = HD // 2
    freq = theta_base ** (-(jnp.arange(half, dtype=jnp.float32) * (2.0 / HD)))
    angles = offset[:, None] * freq[None, :]
    return (segment, places, jnp.cos(angles), jnp.sin(angles))


def rotate(values, cosine, sine):
    half = values.shape[-1] // 2
    first, second = (values[..., :half], values[..., half:])
    cosine = cosine[:, :, None, :]
    sine = sine[:, :, None, :]
    return jnp.concatenate(
        [first * cosine - second * sine, second * cosine + first * sine], axis=-1
    )


def unrotate(grads, cosine, sine):
    half = grads.shape[-1] // 2
    first, second = (grads[..., :half], grads[..., half:])
    cosine = cosine[:, :, None, :]
    sine = sine[:, :, None, :]
    return jnp.concatenate(
        [first * cosine + second * sine, second * cosine - first * sine], axis=-1
    )


def norm_fwd(hidden, gain):
    scale = lax.rsqrt(jnp.mean(hidden * hidden, axis=-1, keepdims=True) + eps_norm)
    return (scale, hidden * scale * gain.astype(jnp.float32))


def norm_bwd(dnormed, hidden, scale, gain):
    gain_f = gain.astype(jnp.float32)
    dgain = jnp.sum(dnormed * hidden * scale, axis=0)
    inner = dnormed * gain_f
    dhidden = scale * inner - hidden * (scale * scale * scale) * jnp.mean(
        inner * hidden, axis=-1, keepdims=True
    )
    return (dhidden, dgain)


def scores_of(query, keys, segment, places):
    raw = jnp.einsum("igha,jga->ghij", query, keys, preferred_element_type=jnp.float32) * (
        1.0 / math.sqrt(HD)
    )
    allowed = (segment[:, None] == segment[None, :]) & (places[None, :] <= places[:, None])
    return jnp.where(allowed[None, None], raw, masked_score)


def attend(query, keys, values, segment, places):
    raw = scores_of(query, keys, segment, places)
    top = jnp.max(raw, axis=-1, keepdims=True)
    total = jnp.sum(jnp.exp(raw - top), axis=-1)
    lse = top[..., 0] + jnp.log(total)
    probs = jnp.exp(raw - lse[..., None]).astype(jnp.bfloat16)
    mixed = jnp.einsum("ghij,jga->igha", probs, values, preferred_element_type=jnp.float32).astype(
        jnp.bfloat16
    )
    return (mixed, lse)


def attend_back(query, keys, values, mixed, dmixed, lse, segment, places):
    raw = scores_of(query, keys, segment, places)
    probs_f = jnp.exp(raw - lse[..., None])
    probs = probs_f.astype(jnp.bfloat16)
    dvals = jnp.einsum("ghij,igha->jga", probs, dmixed, preferred_element_type=jnp.float32)
    dprobs = jnp.einsum("igha,jga->ghij", dmixed, values, preferred_element_type=jnp.float32)
    delta = jnp.einsum("igha,igha->ghi", dmixed, mixed, preferred_element_type=jnp.float32)
    dscores = (probs_f * (dprobs - delta[..., None]) * (1.0 / math.sqrt(HD))).astype(jnp.bfloat16)
    dquery = jnp.einsum("ghij,jga->igha", dscores, keys, preferred_element_type=jnp.float32)
    dkeys = jnp.einsum("ghij,igha->jga", dscores, query, preferred_element_type=jnp.float32)
    return (dquery, dkeys, dvals)


def pad_rows(vector, rows):
    return jnp.pad(vector, (0, rows - vector.shape[0]))


def share_of(weight, index, shards, shares):
    width = weight.shape[1] // shards
    part = width // shares
    return jnp.concatenate(
        [
            lax.dynamic_slice(weight, (0, s * width + index * part), (weight.shape[0], part))
            for s in range(shards)
        ],
        axis=1,
    )


def on_device(
    tokens,
    cotangent,
    lengths,
    query_weight,
    key_weight,
    value_weight,
    output_weight,
    query_bias,
    key_bias,
    value_bias,
    attn_gain,
    gate_weight,
    up_weight,
    down_weight,
    mlp_gain,
):
    shards = lax.axis_size("shard")
    reps = lax.axis_size("rep")
    rep = lax.axis_index("rep")
    rows, width = tokens.shape
    own = query_weight.shape[0]
    kvd = key_weight.shape[1]
    own_kv = key_bias.shape[0]
    small_w = 128
    f32, bf16 = jnp.float32, jnp.bfloat16

    small = jnp.stack(
        [query_bias, attn_gain, mlp_gain, pad_rows(key_bias, own), pad_rows(value_bias, own)],
        axis=1,
    )
    small = jnp.pad(small, ((0, 0), (0, small_w - small.shape[1])))
    packed = jnp.concatenate(
        [query_weight, key_weight, value_weight, output_weight, small], axis=1
    )
    packed = lax.all_gather(packed, "shard", axis=0, tiled=True)
    wide = width + 2 * kvd
    qkv_weight = packed[:, :wide]
    output_full = packed[:, wide : wide + width]
    vectors = packed[:, wide + width : wide + width + 5].T
    query_bias_f, attn_gain_f, mlp_gain_f = vectors[0], vectors[1], vectors[2]
    key_bias_f = vectors[3].reshape(shards, own)[:, :own_kv].reshape(kvd)
    value_bias_f = vectors[4].reshape(shards, own)[:, :own_kv].reshape(kvd)
    qkv_bias = jnp.concatenate([query_bias_f, key_bias_f, value_bias_f]).astype(f32)

    part = down_weight.shape[0] // reps
    gate_mine = lax.all_gather(
        share_of(gate_weight, rep, shards, reps), "shard", axis=0, tiled=True
    )
    up_mine = lax.all_gather(share_of(up_weight, rep, shards, reps), "shard", axis=0, tiled=True)
    down_mine = lax.all_gather(
        lax.dynamic_slice(down_weight, (rep * part, 0), (part, width)),
        "shard",
        axis=0,
        tiled=True,
    )
    cot_all = lax.all_gather(cotangent, "rep", axis=0, tiled=True)

    segment, places, cosine, sine = jax.vmap(lambda lens: tables(lens, rows))(lengths)
    flat = tokens.astype(f32)
    scale_one, normed_one = norm_fwd(flat, attn_gain_f)
    normed_one = normed_one.astype(bf16)
    qkv = jnp.dot(normed_one, qkv_weight, preferred_element_type=f32) + qkv_bias
    query = rotate(qkv[:, :width].reshape(1, rows, HEADS, HD), cosine, sine).astype(bf16)
    query = query.reshape(1, rows, KVH, HEADS // KVH, HD)
    keys = rotate(qkv[:, width : width + kvd].reshape(1, rows, KVH, HD), cosine, sine).astype(bf16)
    values = qkv[:, width + kvd :].reshape(1, rows, KVH, HD).astype(bf16)
    mixed, lse = jax.vmap(attend)(query, keys, values, segment, places)
    mixed_flat = mixed.reshape(rows, width)
    hidden_one = flat + jnp.dot(mixed_flat, output_full, preferred_element_type=f32)
    scale_two, normed_two = norm_fwd(hidden_one, mlp_gain_f)
    normed_all = lax.all_gather(normed_two.astype(bf16), "rep", axis=0, tiled=True)

    gate = jnp.dot(normed_all, gate_mine, preferred_element_type=f32)
    upper = jnp.dot(normed_all, up_mine, preferred_element_type=f32)
    sigma = jax.nn.sigmoid(gate)
    product = (gate * sigma * upper).astype(bf16)
    dprod = times_transposed(cot_all, down_mine)
    dgate = (dprod * upper * sigma * (1.0 + gate * (1.0 - sigma))).astype(bf16)
    dup = (dprod * gate * sigma).astype(bf16)
    dnormed_part = times_transposed(dgate, gate_mine) + times_transposed(dup, up_mine)
    dnormed_two = lax.psum_scatter(
        dnormed_part.astype(bf16), "rep", scatter_dimension=0, tiled=True
    ).astype(f32)
    grad_down = jnp.dot(product.T, cot_all, preferred_element_type=f32).astype(bf16)
    grad_gate = jnp.dot(normed_all.T, dgate, preferred_element_type=f32).astype(bf16)
    grad_up = jnp.dot(normed_all.T, dup, preferred_element_type=f32).astype(bf16)
    down_owned = lax.psum_scatter(grad_down, "shard", scatter_dimension=0, tiled=True)
    gate_owned = lax.psum_scatter(grad_gate, "shard", scatter_dimension=0, tiled=True)
    up_owned = lax.psum_scatter(grad_up, "shard", scatter_dimension=0, tiled=True)
    out_part = jnp.dot(product, down_mine, preferred_element_type=f32).astype(bf16)
    out_sum = lax.psum_scatter(out_part, "rep", scatter_dimension=0, tiled=True)
    result = (hidden_one + out_sum.astype(f32)).astype(bf16)

    dh_two, grad_mlp_gain = norm_bwd(dnormed_two, hidden_one, scale_two, mlp_gain_f)
    dhidden = cotangent.astype(f32) + dh_two
    dres = dhidden.astype(bf16)
    grad_output = jnp.dot(mixed_flat.T, dres, preferred_element_type=f32).astype(bf16)
    dmixed = times_transposed(dres, output_full).astype(bf16)
    dmixed = dmixed.reshape(1, rows, KVH, HEADS // KVH, HD)
    dquery, dkeys, dvals = jax.vmap(attend_back)(
        query, keys, values, mixed, dmixed, lse, segment, places
    )
    dquery = unrotate(dquery.reshape(1, rows, HEADS, HD), cosine, sine).reshape(rows, width)
    dkeys = unrotate(dkeys, cosine, sine).reshape(rows, kvd)
    dvals = dvals.reshape(rows, kvd)
    dqkv = jnp.concatenate([dquery, dkeys, dvals], axis=1)
    grad_bias = jnp.sum(dqkv, axis=0)
    dqkv_b = dqkv.astype(bf16)
    grad_qkv = jnp.dot(normed_one.T, dqkv_b, preferred_element_type=f32).astype(bf16)
    dnormed_one = times_transposed(dqkv_b, qkv_weight)
    dh_one, grad_attn_gain = norm_bwd(dnormed_one, flat, scale_one, attn_gain_f)
    grad_input = dhidden + dh_one

    spread = lambda v: jnp.pad(
        v.reshape(shards, own_kv), ((0, 0), (0, own - own_kv))
    ).reshape(width)
    small_g = jnp.stack(
        [
            grad_bias[:width],
            grad_attn_gain,
            grad_mlp_gain,
            spread(grad_bias[width : width + kvd]),
            spread(grad_bias[width + kvd :]),
        ],
        axis=0,
    )
    small_g = jnp.pad(small_g, ((0, small_w - small_g.shape[0]), (0, 0))).T.astype(bf16)
    packed_g = jnp.concatenate([grad_qkv, grad_output, small_g], axis=1)
    owned = lax.psum_scatter(packed_g, "shard", scatter_dimension=0, tiled=True)
    total_w = wide + width
    share_w = total_w // reps
    chunks = [
        jnp.concatenate([owned[:, i * share_w : (i + 1) * share_w], owned[:, total_w:]], axis=1)
        for i in range(reps)
    ]
    split = lax.psum_scatter(
        jnp.concatenate(chunks, axis=0), "rep", scatter_dimension=0, tiled=True
    )
    vec = split[:, share_w : share_w + 5].astype(f32).T

    attn_all = lax.all_gather(split[:, :share_w], "rep", axis=0)
    attn_all = jnp.concatenate([attn_all[i] for i in range(reps)], axis=1).astype(f32)
    down_all = lax.all_gather(down_owned, "rep", axis=0, tiled=True).astype(f32)

    def joined(share):
        every = lax.all_gather(share, "rep", axis=0)
        return jnp.concatenate(
            [
                every[r][:, s * part : (s + 1) * part]
                for s in range(shards)
                for r in range(reps)
            ],
            axis=1,
        ).astype(f32)

    return (
        result,
        grad_input,
        attn_all[:, :width],
        attn_all[:, width : width + kvd],
        attn_all[:, width + kvd : wide],
        attn_all[:, wide:],
        vec[0],
        vec[3][:own_kv],
        vec[4][:own_kv],
        vec[1],
        joined(gate_owned),
        joined(up_owned),
        down_all,
        vec[2],
    )


def solution(mesh):
    in_specs = (
        P(("rep", "shard"), None),
        P(("rep", "shard"), None),
        P(("rep", "shard"), None),
        P("shard", None),
        P("shard", None),
        P("shard", None),
        P("shard", None),
        P("shard"),
        P("shard"),
        P("shard"),
        P("shard"),
        P("shard", None),
        P("shard", None),
        P("shard", None),
        P("shard"),
    )
    out_specs = (
        P(("rep", "shard"), None),
        P(("rep", "shard"), None),
        P("shard", None),
        P("shard", None),
        P("shard", None),
        P("shard", None),
        P("shard"),
        P("shard"),
        P("shard"),
        P("shard"),
        P("shard", None),
        P("shard", None),
        P("shard", None),
        P("shard"),
    )
    return jax.shard_map(
        on_device, mesh=mesh, in_specs=in_specs, out_specs=out_specs, check_vma=False
    )
```

time: 1500 us -> 712 us (0.47)
  waiting for transfers between devices: 1190 us -> 569 us
  blocking collectives: 154 us -> 27.6 us
  matrix products: 83.1 us -> 49 us
    reduce_scatter x7 -> x6, waiting for transfers between devices: 688 us -> 271 us  [the longest x1 86.8 us: on_device(): owned = lax.psum_scatter(packed_g, 'shard', scatter_dimension=0, tiled=True)]
    all_gather x8 -> x7, waiting for transfers between devices: 414 us -> 220 us  [the longest x1 55.2 us: on_device(): packed = lax.all_gather(packed, 'shard', axis=0, tiled=True)]
    unnamed x3 -> x0, blocking collectives: 62.9 us -> none
    all_gather x6 -> x3, blocking collectives: 84.9 us -> 27.6 us  [the longest x1 11.2 us: on_device(): cot_all = lax.all_gather(cotangent, 'rep', axis=0, tiled=True)]
    unnamed x121 -> x31, local copies, waits for them, and re-layouts: 26.6 us -> 6.93 us
    dot_general x14 -> x10, matrix products: 48.6 us -> 33.2 us  [the longest x1 4.96 us: on_device(): upper = jnp.dot(normed_all, up_mine, preferred_element_type=f32)]
    unnamed x29 -> x15, waiting for transfers between devices: 90.3 us -> 78 us
  transfers between devices with their start and end apart: 22 -> 14, of which waited for: 18 -> 14; matrix products, arithmetic and copies ran while one was open for 7% -> 10% of each run, Pallas kernels for 0% -> 0%
where the time goes in v1:
time: 712 us; the launch traced here: 711 us
  waiting for transfers between devices  569 us (80%)
  matrix products  49 us (7%)
  local copies, waits for them, and re-layouts  33.5 us (5%)
  blocking collectives  27.6 us (4%)
  other arithmetic  16.8 us (2%)
  between operations  14.4 us (2%)
    reduce_scatter x1, waiting for transfers between devices, on_device(): owned = lax.psum_scatter(packed_g, 'shard', scatter_dimension=0, tiled=True)  86.8 us
    unnamed x15, waiting for transfers between devices  78 us
    reduce_scatter x1, waiting for transfers between devices, on_device(): lax.psum_scatter(grad_gate, 'shard', scatter_dimension=0, tiled=True)  72.2 us
    reduce_scatter x1, waiting for transfers between devices, on_device(): lax.psum_scatter(grad_up, 'shard', scatter_dimension=0, tiled=True)  60.8 us
    all_gather x1, waiting for transfers between devices, on_device(): packed = lax.all_gather(packed, 'shard', axis=0, tiled=True)  55.2 us
    all_gather x1, waiting for transfers between devices, on_device(): lax.all_gather(share_of(up_weight, rep, shards, reps), 'shard', axis=0, t...  47.5 us
    all_gather x1, waiting for transfers between devices, on_device(): lax.all_gather(lax.dynamic_slice(down_weight, (rep * part, 0), (part, wid...  46.3 us
    all_gather x1, waiting for transfers between devices, on_device(): lax.all_gather(share_of(gate_weight, rep, shards, reps), 'shard', axis=0,...  34.8 us
  transfers between devices with their start and end apart: 14, of which 14 were waited for; matrix products, arithmetic and copies ran while one was open for 10% of the time, Pallas kernels for 0%

profile of v1, /device:TPU:0, one launch (start us, length us, event | category | flops | bytes accessed | tf_op | source)
XLA Modules:
  0.0 711.2 jit_solution(1980135578788501737)
XLA Ops:
  8.8 0.9 constant_dynamic-update-slice_fusion.3
  11.3 1.0 constant_dynamic-update-slice_fusion
  13.2 1.9 constant_dynamic-slice_fusion.1
  15.1 0.9 concatenate.94
  16.1 0.9 concatenate.95
  18.5 11.2 %all_gather.44 = bf16[512,896]{1,0:T(8,128)(2,1)} all-gather(bf16[128,896]{1,0:T(8,128)(2,1)S(1)} %copy-done.7), channel_id=1, replica_groups=mesh['rep'=4,'shard'=8] {'rep'}, dimensions={0}, use_global_device_ids=true | all-gather | bytes 1146880 | tf_op jit(solution)/shard_map/all_gather | solution.py:181
  29.9 55.2 %all-gather.11.cloned.1.call-done = bf16[896,2176]{1,0:T(8,128)(2,1)} async-done(((bf16[112,2176]{1,0:T(8,128)(2,1)}), bf16[896,2176]{1,0:T(8,128)(2,1)}) %all-gather.11.cloned.1.call-update) | async-done | bytes 3899408 | tf_op jit(solution)/shard_map/all_gather | solution.py:160
  85.1 1.0 slice_bitcast_fusion
  87.2 2.1 convolution_add_fusion
  90.7 2.0 multiply_reduce_fusion
  92.8 9.9 %all_gather.40 = bf16[512,896]{1,0:T(8,128)(2,1)} all-gather(bf16[128,896]{1,0:T(8,128)(2,1)S(1)} %multiply_convert_fusion.3), channel_id=1, replica_groups=mesh['rep'=4,'shard'=8] {'rep'}, dimensions={0}, use_global_device_ids=true | all-gather | bytes 1146880 | tf_op jit(solution)/shard_map/all_gather | solution.py:196
  102.7 34.8 %all-gather.13.cloned.1.call-done = bf16[896,1216]{1,0:T(8,128)(2,1)} async-done(((bf16[112,1216]{1,0:T(8,128)(2,1)}), bf16[896,1216]{1,0:T(8,128)(2,1)}) %all-gather.13.cloned.1.call-update) | async-done | bytes 2179088 | tf_op jit(solution)/shard_map/all_gather | solution.py:171
  137.5 4.9 fusion.66
  142.4 47.5 %all-gather.15.cloned.1.call-done = bf16[896,1216]{1,0:T(8,128)(2,1)} async-done(((bf16[112,1216]{1,0:T(8,128)(2,1)}), bf16[896,1216]{1,0:T(8,128)(2,1)}) %all-gather.15.cloned.1.call-update) | async-done | bytes 2179088 | tf_op jit(solution)/shard_map/all_gather | solution.py:174
  189.8 5.0 fusion.67
  194.8 46.3 %all-gather.17.cloned.1.call-done = bf16[1216,896]{1,0:T(8,128)(2,1)} async-done(((bf16[152,896]{1,0:T(8,128)(2,1)}), bf16[1216,896]{1,0:T(8,128)(2,1)}) %all-gather.17.cloned.1.call-update) | async-done | bytes 2179088 | tf_op jit(solution)/shard_map/all_gather | solution.py:175
  241.1 7.0 multiply_convert_fusion
  248.1 1.6 fusion.68
  250.7 2.6 add_convert_fusion
  253.3 4.5 convolution_convert_fusion.5
  257.9 4.5 convolution_convert_fusion.1
  262.5 4.4 convolution_convert_fusion.2
  267.1 4.5 convolution_convert_fusion
  271.7 4.2 reduce-scatter.12.cloned.1.call-done
  275.9 1.1 fusion.27
  277.1 25.3 %reduce-scatter.10.cloned.1.call-done = bf16[128,896]{1,0:T(8,128)(2,1)} async-done(((bf16[512,896]{1,0:T(8,128)(2,1)}), bf16[128,896]{1,0:T(8,128)(2,1)}) %reduce-scatter.10.cloned.1.call-update) | async-done | bytes 229392 | tf_op jit(solution)/shard_map/reduce_scatter | solution.py:216
  302.4 1.9 fusion.24
  304.3 2.0 fusion.17
  308.0 1.4 copy-done.3
  312.7 2.1 pad_maximum_fusion
  314.8 60.8 %reduce-scatter.20.cloned.1.call-done = bf16[112,1216]{1,0:T(8,128)(2,1)} async-done(((bf16[896,1216]{1,0:T(8,128)(2,1)}), bf16[112,1216]{1,0:T(8,128)(2,1)}) %reduce-scatter.20.cloned.1.call-update) | async-done | bytes 272400 | tf_op jit(solution)/shard_map/reduce_scatter | solution.py:214
  375.7 72.2 %reduce-scatter.18.cloned.1.call-done = bf16[112,1216]{1,0:T(8,128)(2,1)} async-done(((bf16[896,1216]{1,0:T(8,128)(2,1)}), bf16[112,1216]{1,0:T(8,128)(2,1)}) %reduce-scatter.18.cloned.1.call-update) | async-done | bytes 272400 | tf_op jit(solution)/shard_map/reduce_scatter | solution.py:213
  448.0 77.8 %reduce-scatter.22.cloned.1.call-done = bf16[152,896]{1,0:T(8,128)(2,1)} async-done(((bf16[1216,896]{1,0:T(8,128)(2,1)}), bf16[152,896]{1,0:T(8,128)(2,1)}) %reduce-scatter.22.cloned.1.call-update) | async-done | bytes 272400
  525.8 86.8 %reduce-scatter.14.cloned.1.call-done = bf16[112,2176]{1,0:T(8,128)(2,1)} async-done(((bf16[896,2176]{1,0:T(8,128)(2,1)}), bf16[112,2176]{1,0:T(8,128)(2,1)}) %reduce-scatter.14.cloned.1.call-update) | async-done | bytes 487440 | tf_op jit(solution)/shard_map/reduce_scatter | solution.py:254
  614.3 1.0 fusion.62
  616.3 1.0 fusion.34
  617.2 14.0 %all-gather.23.cloned.1.call-done = bf16[448,1216]{1,0:T(8,128)(2,1)} async-done(((bf16[112,1216]{1,0:T(8,128)(2,1)}), bf16[448,1216]{1,0:T(8,128)(2,1)}) %all-gather.23.cloned.1.call-update) | async-done | bytes 1089552 | tf_op jit(solution)/shard_map/all_gather | solution.py:271
  631.2 1.6 fusion.59
  633.3 3.9 concatenate.107
  637.2 1.5 convert_element_type.175
  638.7 11.2 %all-gather.21.cloned.1.call-done = bf16[448,1216]{1,0:T(8,128)(2,1)} async-done(((bf16[112,1216]{1,0:T(8,128)(2,1)}), bf16[448,1216]{1,0:T(8,128)(2,1)}) %all-gather.21.cloned.1.call-update) | async-done | bytes 1089552 | tf_op jit(solution)/shard_map/all_gather | solution.py:271
  649.9 1.6 fusion.61
  652.0 3.8 concatenate.106
  655.9 1.5 convert_element_type.173
  657.4 11.1 %all-gather.19.cloned.1.call-done = bf16[608,896]{1,0:T(8,128)(2,1)} async-done(((bf16[152,896]{1,0:T(8,128)(2,1)}), bf16[608,896]{1,0:T(8,128)(2,1)}) %all-gather.19.cloned.1.call-update) | async-done | bytes 1089552 | tf_op jit(solution)/shard_map/all_gather | solution.py:268
  668.4 2.7 convert_element_type.177
  671.2 21.6 %reduce-scatter.16.cloned.1.call-done = bf16[112,640]{1,0:T(8,128)(2,1)} async-done(((bf16[448,640]{1,0:T(8,128)(2,1)}), bf16[112,640]{1,0:T(8,128)(2,1)}) %reduce-scatter.16.cloned.1.call-update) | async-done | bytes 143376 | tf_op jit(solution)/shard_map/reduce_scatter | solution.py:261
  695.9 6.5 all-gather
  (134 shorter events, 23.7 us)
Async XLA Ops:
  7.2 9.9 %copy-start = (bf16[608,896]{1,0:T(8,128)(2,1)S(1)}, bf16[608,896]{1,0:T(8,128)(2,1)}, u32[]{:S(2)}) copy-start(bf16[608,896]{1,0:T(8,128)(2,1)} %param.28) | copy-start | bytes 3268612
  7.2 77.9 %all-gather.11.cloned.1.call-start = ((), (), s32[]{:S(2)}) async-start(), calls=%async_computation.7 | async-start | bytes 4386816 | tf_op jit(solution)/shard_map/all_gather | solution.py:160
  12.3 0.8 copy-start.6
  13.1 124.4 %all-gather.13.cloned.1.call-start = ((), (), s32[]{:S(2)}) async-start(), calls=%async_computation.8 | async-start | bytes 2580480 | tf_op jit(solution)/shard_map/all_gather | solution.py:171
  13.2 4.8 copy-start.10
  13.2 5.1 copy-start.2
  13.2 5.3 copy-start.7
  16.0 173.8 %all-gather.15.cloned.1.call-start = ((), (), s32[]{:S(2)}) async-start(), calls=%async_computation.9 | async-start | bytes 2580480 | tf_op jit(solution)/shard_map/all_gather | solution.py:174
  17.1 224.0 %all-gather.17.cloned.1.call-start = ((), (), s32[]{:S(2)}) async-start(), calls=%async_computation.10 | async-start | bytes 2451456 | tf_op jit(solution)/shard_map/all_gather | solution.py:175
  17.9 258.0 %reduce-scatter.12.cloned.1.call-start = ((), (), s32[]{:S(2)}) async-start(), calls=%async_computation.12 | async-start | bytes 1146880 | tf_op jit(solution)/shard_map/reduce_scatter | solution.py:206
  241.1 7.0 copy-start.8
  248.1 1.6 copy-start.11
  248.1 1.6 copy-start.12
  248.1 2.5 copy-start.9
  253.3 49.1 %reduce-scatter.10.cloned.1.call-start = ((), (), s32[]{:S(2)}) async-start(), calls=%async_computation.11 | async-start | bytes 1146880 | tf_op jit(solution)/shard_map/reduce_scatter | solution.py:216
  257.8 117.8 %reduce-scatter.20.cloned.1.call-start = ((), (), s32[]{:S(2)}) async-start(), calls=%async_computation.16 | async-start | bytes 2580480 | tf_op jit(solution)/shard_map/reduce_scatter | solution.py:214
  262.4 185.5 %reduce-scatter.18.cloned.1.call-start = ((), (), s32[]{:S(2)}) async-start(), calls=%async_computation.15 | async-start | bytes 2580480 | tf_op jit(solution)/shard_map/reduce_scatter | solution.py:213
  266.9 258.9 %reduce-scatter.22.cloned.1.call-start = ((), (), s32[]{:S(2)}) async-start(), calls=%async_computation.20 | async-start | bytes 2451456
  271.6 341.0 %reduce-scatter.14.cloned.1.call-start = ((), (), s32[]{:S(2)}) async-start(), calls=%async_computation.13 | async-start | bytes 4386816 | tf_op jit(solution)/shard_map/reduce_scatter | solution.py:254
  307.3 2.1 copy-start.3
  314.7 316.5 %all-gather.23.cloned.1.call-start = ((), (), s32[]{:S(2)}) async-start(), calls=%async_computation.19 | async-start | bytes 1433600 | tf_op jit(solution)/shard_map/all_gather | solution.py:271
  375.6 274.3 %all-gather.21.cloned.1.call-start = ((), (), s32[]{:S(2)}) async-start(), calls=%async_computation.18 | async-start | bytes 1433600 | tf_op jit(solution)/shard_map/all_gather | solution.py:271
  447.9 220.5 %all-gather.19.cloned.1.call-start = ((), (), s32[]{:S(2)}) async-start(), calls=%async_computation.17 | async-start | bytes 1361920 | tf_op jit(solution)/shard_map/all_gather | solution.py:268
  525.8 167.0 %reduce-scatter.16.cloned.1.call-start = ((), (), s32[]{:S(2)}) async-start(), calls=%async_computation.14 | async-start | bytes 716800 | tf_op jit(solution)/shard_map/reduce_scatter | solution.py:261
  631.2 1.7 copy-start.5
  649.9 1.7 copy-start.4
  695.8 8.8 %copy-start.1 = (bf16[608,896]{1,0:T(8,128)(2,1)S(1)}, bf16[608,896]{1,0:T(8,128)(2,1)}, u32[]{:S(2)}) copy-start(bf16[608,896]{1,0:T(8,128)(2,1)} %param.28) | copy-start | bytes 3268612
Sparse Core Ops, SparseCore 0:
  13.2 71.7 all-gather.10
  87.8 49.6 all-gather.12
  140.3 49.5 all-gather.14
  192.5 48.5 all-gather.16
  253.4 22.4 reduce-scatter.11
  278.3 23.9 reduce-scatter.9
  305.9 69.6 reduce-scatter.19
  379.1 68.7 reduce-scatter.17
  451.9 73.7 reduce-scatter.21
  529.1 83.4 reduce-scatter.13
  614.2 16.9 all-gather.22
  632.6 17.2 all-gather.20
  651.5 16.9 all-gather.18
  670.8 21.9 reduce-scatter.15

commit v2 on v1

--- a/solution.py
+++ b/solution.py
@@ -120,6 +120,29 @@
         ],
         axis=1,
     )
+
+
+def row_pieces(array, count):
+    rows = array.shape[0]
+    step = -(-rows // count)
+    step = min(rows, -(-step // 8) * 8)
+    return [array[i : min(i + step, rows)] for i in range(0, rows, step)]
+
+
+def fold(blocks, wide):
+    count, rows, cols = blocks.shape
+    if rows % 8 or cols % 128 or (rows // 8) * 128 != wide:
+        return blocks.reshape(count, rows * cols // wide, wide)
+    tiles = blocks.reshape(count, rows // 8, 8, cols // 128, 128)
+    return tiles.transpose(0, 3, 2, 1, 4).reshape(count, cols // 16, wide)
+
+
+def unfold(blocks, rows, cols):
+    count, _, wide = blocks.shape
+    if rows % 8 or cols % 128 or (rows // 8) * 128 != wide:
+        return blocks.reshape(count, rows, cols)
+    tiles = blocks.reshape(count, cols // 128, 8, rows // 8, 128)
+    return tiles.transpose(0, 3, 2, 1, 4).reshape(count, rows, cols)
 
 
 def on_device(
@@ -168,16 +191,19 @@
     qkv_bias = jnp.concatenate([query_bias_f, key_bias_f, value_bias_f]).astype(f32)
 
     part = down_weight.shape[0] // reps
-    gate_mine = lax.all_gather(
-        share_of(gate_weight, rep, shards, reps), "shard", axis=0, tiled=True
-    )
-    up_mine = lax.all_gather(share_of(up_weight, rep, shards, reps), "shard", axis=0, tiled=True)
-    down_mine = lax.all_gather(
-        lax.dynamic_slice(down_weight, (rep * part, 0), (part, width)),
+    both_mine = lax.all_gather(
+        jnp.concatenate(
+            [share_of(gate_weight, rep, shards, reps), share_of(up_weight, rep, shards, reps)],
+            axis=1,
+        ),
         "shard",
         axis=0,
         tiled=True,
     )
+    down_part = lax.dynamic_slice(down_weight, (rep * part, 0), (part, width))
+    down_mine = jnp.concatenate(
+        [lax.all_gather(p, "shard", axis=0) for p in row_pieces(down_part, 3)], axis=1
+    ).reshape(shards * part, width)
     cot_all = lax.all_gather(cotangent, "rep", axis=0, tiled=True)
 
     segment, places, cosine, sine = jax.vmap(lambda lens: tables(lens, rows))(lengths)
@@ -195,26 +221,37 @@
     scale_two, normed_two = norm_fwd(hidden_one, mlp_gain_f)
     normed_all = lax.all_gather(normed_two.astype(bf16), "rep", axis=0, tiled=True)
 
-    gate = jnp.dot(normed_all, gate_mine, preferred_element_type=f32)
-    upper = jnp.dot(normed_all, up_mine, preferred_element_type=f32)
+    both = jnp.dot(normed_all, both_mine, preferred_element_type=f32)
+    hidden = both.shape[1] // 2
+    gate, upper = both[:, :hidden], both[:, hidden:]
     sigma = jax.nn.sigmoid(gate)
     product = (gate * sigma * upper).astype(bf16)
     dprod = times_transposed(cot_all, down_mine)
     dgate = (dprod * upper * sigma * (1.0 + gate * (1.0 - sigma))).astype(bf16)
     dup = (dprod * gate * sigma).astype(bf16)
-    dnormed_part = times_transposed(dgate, gate_mine) + times_transposed(dup, up_mine)
-    dnormed_two = lax.psum_scatter(
-        dnormed_part.astype(bf16), "rep", scatter_dimension=0, tiled=True
+    dboth = jnp.concatenate([dgate, dup], axis=1)
+    dnormed_part = times_transposed(dboth, both_mine).astype(bf16)
+    out_part = jnp.dot(product, down_mine, preferred_element_type=f32).astype(bf16)
+    sums = lax.psum_scatter(
+        jnp.concatenate([dnormed_part, out_part], axis=1), "rep", scatter_dimension=0, tiled=True
     ).astype(f32)
+    dnormed_two, out_sum = sums[:, :width], sums[:, width:]
+    result = (hidden_one + out_sum).astype(bf16)
     grad_down = jnp.dot(product.T, cot_all, preferred_element_type=f32).astype(bf16)
-    grad_gate = jnp.dot(normed_all.T, dgate, preferred_element_type=f32).astype(bf16)
-    grad_up = jnp.dot(normed_all.T, dup, preferred_element_type=f32).astype(bf16)
-    down_owned = lax.psum_scatter(grad_down, "shard", scatter_dimension=0, tiled=True)
-    gate_owned = lax.psum_scatter(grad_gate, "shard", scatter_dimension=0, tiled=True)
-    up_owned = lax.psum_scatter(grad_up, "shard", scatter_dimension=0, tiled=True)
-    out_part = jnp.dot(product, down_mine, preferred_element_type=f32).astype(bf16)
-    out_sum = lax.psum_scatter(out_part, "rep", scatter_dimension=0, tiled=True)
-    result = (hidden_one + out_sum.astype(f32)).astype(bf16)
+    grad_both = jnp.dot(normed_all.T, dboth, preferred_element_type=f32).astype(bf16)
+    mlp_owned = lax.psum_scatter(
+        jnp.concatenate(
+            [
+                grad_both.reshape(shards, own, 2 * hidden),
+                fold(grad_down.reshape(shards, part, width), 2 * hidden),
+            ],
+            axis=1,
+        ).reshape(-1, 2 * hidden),
+        "shard",
+        scatter_dimension=0,
+        tiled=True,
+    )
+    mlp_owned = lax.optimization_barrier(mlp_owned)
 
     dh_two, grad_mlp_gain = norm_bwd(dnormed_two, hidden_one, scale_two, mlp_gain_f)
     dhidden = cotangent.astype(f32) + dh_two
@@ -265,13 +302,22 @@
 
     attn_all = lax.all_gather(split[:, :share_w], "rep", axis=0)
     attn_all = jnp.concatenate([attn_all[i] for i in range(reps)], axis=1).astype(f32)
-    down_all = lax.all_gather(down_owned, "rep", axis=0, tiled=True).astype(f32)
-
-    def joined(share):
-        every = lax.all_gather(share, "rep", axis=0)
+
+    def from_replicas(share):
+        limit = max(1, (240 * 1024) // (2 * share.shape[1]))
+        count = -(-share.shape[0] // limit)
+        return jnp.concatenate(
+            [lax.all_gather(p, "rep", axis=0) for p in row_pieces(share, count)], axis=1
+        )
+
+    both_all = from_replicas(mlp_owned[:own])
+    down_all = unfold(from_replicas(mlp_owned[own:]), part, width)
+    down_all = down_all.reshape(reps * part, width).astype(f32)
+
+    def joined(first):
         return jnp.concatenate(
             [
-                every[r][:, s * part : (s + 1) * part]
+                both_all[r][:, first + s * part : first + (s + 1) * part]
                 for s in range(shards)
                 for r in range(reps)
             ],
@@ -289,8 +335,8 @@
         vec[3][:own_kv],
         vec[4][:own_kv],
         vec[1],
-        joined(gate_owned),
-        joined(up_owned),
+        joined(0),
+        joined(hidden),
         down_all,
         vec[2],
     )

time: 712 us -> 547 us (0.77)
  waiting for transfers between devices: 569 us -> 266 us
  blocking collectives: 27.6 us -> 170 us
  matrix products: 49 us -> 30 us
  other arithmetic: 16.8 us -> 25.5 us
    all_gather x0 -> x8, blocking collectives: none -> 144 us  [the longest x3 104 us: on_device(): lax.all_gather(p, 'shard', axis=0)]
    reduce_scatter x4 -> x1, waiting for transfers between devices: 163 us -> 28 us  [on_device(): lax.psum_scatter(jnp.concatenate([dnormed_part, out_part], axis=1), 'rep'...]
    all_gather x6 -> x1, waiting for transfers between devices: 165 us -> 33.1 us  [on_device(): lax.all_gather(jnp.concatenate([share_of(gate_weight, rep, shards, reps),...]
    all_gather x1, waiting for transfers between devices: 55.2 us -> 0.01 us  [on_device(): packed = lax.all_gather(packed, 'shard', axis=0, tiled=True)]
    unnamed x15 -> x7, waiting for transfers between devices: 78 us -> 114 us
    reduce_scatter x1, waiting for transfers between devices: 21.6 us -> 6.5 us  [on_device(): lax.psum_scatter(jnp.concatenate(chunks, axis=0), 'rep', scatter_dimensio...]
    dot_general x4 -> x2, matrix products: 18.7 us -> 10.2 us  [the longest x1 5.51 us: on_device(): both = jnp.dot(normed_all, both_mine, preferred_element_type=f32)]
    concatenate x0 -> x4, other arithmetic: none -> 8.46 us  [the longest x1 5.43 us: on_device(): jnp.concatenate([grad_both.reshape(shards, own, 2 * hidden), fold(grad_do...]
  transfers between devices with their start and end apart: 14 -> 6, of which waited for: 14 -> 5; matrix products, arithmetic and copies ran while one was open for 10% -> 6% of each run, Pallas kernels for 0% -> 0%
where the time goes in v2:
time: 547 us; the launch traced here: 545 us
  waiting for transfers between devices  266 us (49%)
  blocking collectives  170 us (31%)
  local copies, waits for them, and re-layouts  38.8 us (7%)
  matrix products  30 us (5%)
  other arithmetic  25.5 us (5%)
  between operations  15 us (3%)
    unnamed x7, waiting for transfers between devices  114 us
    all_gather x3, blocking collectives, on_device(): lax.all_gather(p, 'shard', axis=0)  104 us
    reduce_scatter x1, waiting for transfers between devices, on_device(): owned = lax.psum_scatter(packed_g, 'shard', scatter_dimension=0, tiled=True)  84.4 us
    all_gather x5, blocking collectives, from_replicas(): lax.all_gather(p, 'rep', axis=0)  40 us
    all_gather x1, waiting for transfers between devices, on_device(): lax.all_gather(jnp.concatenate([share_of(gate_weight, rep, shards, reps),...  33.1 us
    reduce_scatter x1, waiting for transfers between devices, on_device(): lax.psum_scatter(jnp.concatenate([dnormed_part, out_part], axis=1), 'rep'...  28 us
  transfers between devices with their start and end apart: 6, of which 5 were waited for; matrix products, arithmetic and copies ran while one was open for 6% of the time, Pallas kernels for 0%

profile of v2, /device:TPU:0, one launch (start us, length us, event | category | flops | bytes accessed | tf_op | source)
XLA Modules:
  0.0 545.3 jit_solution(5100568708691602963)
XLA Ops:
  13.1 1.9 constant_dynamic-slice_fusion.2
  14.9 1.3 concatenate.110
  18.6 35.2 %all-gather.2 = bf16[320,896]{1,0:T(8,128)(2,1)S(1)} all-gather(bf16[40,896]{1,0:T(8,128)(2,1)S(1)} %constant_dynamic-slice_fusion.18), channel_id=4, replica_groups=mesh['rep'=4,'shard'=8] {'shard'}, dimensions={0}, use_global_device_ids=true | all-gather | bytes 645120 | tf_op jit(solution)/shard_map/all_gather | solution.py:205
  53.8 34.7 %all-gather = bf16[448,896]{1,0:T(8,128)(2,1)S(1)} all-gather(bf16[56,896]{1,0:T(8,128)(2,1)S(1)} %get-tuple-element.39), channel_id=2, replica_groups=mesh['rep'=4,'shard'=8] {'shard'}, dimensions={0}, use_global_device_ids=true | all-gather | bytes 903168 | tf_op jit(solution)/shard_map/all_gather | solution.py:205
  88.6 33.8 %all-gather.1 = bf16[448,896]{1,0:T(8,128)(2,1)S(1)} all-gather(bf16[56,896]{1,0:T(8,128)(2,1)S(1)} %get-tuple-element.40), channel_id=3, replica_groups=mesh['rep'=4,'shard'=8] {'shard'}, dimensions={0}, use_global_device_ids=true | all-gather | bytes 903168 | tf_op jit(solution)/shard_map/all_gather | solution.py:205
  122.3 1.5 pad_maximum_fusion.3
  124.6 9.6 %all_gather.73 = bf16[512,896]{1,0:T(8,128)(2,1)S(1)} all-gather(bf16[128,896]{1,0:T(8,128)(2,1)S(1)} %copy-done.4), channel_id=1, replica_groups=mesh['rep'=4,'shard'=8] {'rep'}, dimensions={0}, use_global_device_ids=true | all-gather | bytes 1146880 | tf_op jit(solution)/shard_map/all_gather | solution.py:207
  134.2 1.2 slice_bitcast_fusion.4
  137.1 2.1 convolution_add_fusion
  141.1 2.0 multiply_reduce_fusion.2
  143.7 10.1 %all_gather.74 = bf16[512,896]{1,0:T(8,128)(2,1)} all-gather(bf16[128,896]{1,0:T(8,128)(2,1)S(1)} %multiply_convert_fusion.3), channel_id=1, replica_groups=mesh['rep'=4,'shard'=8] {'rep'}, dimensions={0}, use_global_device_ids=true | all-gather | bytes 1146880 | tf_op jit(solution)/shard_map/all_gather | solution.py:222
  153.8 33.1 %all-gather.14.cloned.1.call-done = bf16[896,2432]{1,0:T(8,128)(2,1)} async-done(((bf16[112,2432]{1,0:T(8,128)(2,1)}), bf16[896,2432]{1,0:T(8,128)(2,1)}) %all-gather.14.cloned.1.call-update) | async-done | bytes 4358160 | tf_op jit(solution)/shard_map/all_gather | solution.py:194
  186.9 5.5 %fusion.66 = f32[512,2432]{0,1:T(8,128)S(1)} fusion(bf16[512,896]{1,0:T(8,128)(2,1)} %all_gather.74, bf16[896,2432]{1,0:T(8,128)(2,1)} %all-gather.14.cloned.1.call-done), kind=kOutput, calls=%fused_computation.175 | convolution fusion | flops 2231369728 | bytes 10256384 | tf_op jit(solution)/shard_map/dot_general | solution.py:224
  192.5 2.5 multiply_convert_fusion.2
  195.1 1.6 convolution_convert_fusion.4
  196.7 2.9 fusion.4
  199.6 1.4 pad_maximum_fusion.5
  201.2 28.0 %reduce-scatter.7.cloned.1.call-done = bf16[128,1792]{1,0:T(8,128)(2,1)} async-done(((bf16[512,1792]{1,0:T(8,128)(2,1)}), bf16[128,1792]{1,0:T(8,128)(2,1)}) %reduce-scatter.7.cloned.1.call-update) | async-done | bytes 458768 | tf_op jit(solution)/shard_map/reduce_scatter | solution.py:235
  229.2 1.1 convert_element_type.163
  231.0 1.5 subtract_add_fusion
  232.5 2.0 fusion.19
  236.6 1.7 convolution_convert_fusion.3
  240.9 3.2 pad_maximum_fusion.1
  244.2 84.4 %reduce-scatter.9.cloned.1.call-done = bf16[112,2176]{1,0:T(8,128)(2,1)} async-done(((bf16[896,2176]{1,0:T(8,128)(2,1)}), bf16[112,2176]{1,0:T(8,128)(2,1)}) %reduce-scatter.9.cloned.1.call-update) | async-done | bytes 487440 | tf_op jit(solution)/shard_map/reduce_scatter | solution.py:291
  330.2 1.0 fusion.62
  332.2 1.5 convolution_convert_fusion.1
  335.7 4.7 convolution_convert_fusion
  340.4 5.4 pad_maximum_fusion
  346.4 1.0 fusion.29
  347.4 6.5 %reduce-scatter.11.cloned.1.call-done = bf16[112,640]{1,0:T(8,128)(2,1)} async-done(((bf16[448,640]{1,0:T(8,128)(2,1)}), bf16[112,640]{1,0:T(8,128)(2,1)}) %reduce-scatter.11.cloned.1.call-update) | async-done | bytes 143376 | tf_op jit(solution)/shard_map/reduce_scatter | solution.py:298
  354.8 6.3 %all-gather.3 = bf16[448,512]{1,0:T(8,128)(2,1)S(1)} all-gather(bf16[112,512]{1,0:T(8,128)(2,1)S(1)} %slice.630), channel_id=5, replica_groups=mesh['rep'=4,'shard'=8] {'rep'}, dimensions={0}, use_global_device_ids=true | all-gather | bytes 573440 | tf_op jit(solution)/shard_map/all_gather | solution.py:303
  365.6 113.8 %reduce-scatter.13.cloned.1.call-done = bf16[168,2432]{1,0:T(8,128)(2,1)} async-done(((bf16[1344,2432]{1,0:T(8,128)(2,1)}), bf16[168,2432]{1,0:T(8,128)(2,1)}) %reduce-scatter.13.cloned.1.call-update) | async-done | bytes 817168
  480.3 1.0 fusion.56
  481.3 1.0 fusion.57
  482.4 6.9 %all-gather.8 = bf16[96,2432]{1,0:T(8,128)(2,1)S(1)} all-gather(bf16[24,2432]{1,0:T(8,128)(2,1)S(1)} %slice.713), channel_id=10, replica_groups=mesh['rep'=4,'shard'=8] {'rep'}, dimensions={0}, use_global_device_ids=true | all-gather | bytes 583680 | tf_op jit(solution)/shard_map/all_gather | solution.py:310
  489.2 7.8 %all-gather.7 = bf16[128,2432]{1,0:T(8,128)(2,1)S(1)} all-gather(bf16[32,2432]{1,0:T(8,128)(2,1)S(1)} %get-tuple-element.57), channel_id=9, replica_groups=mesh['rep'=4,'shard'=8] {'rep'}, dimensions={0}, use_global_device_ids=true | all-gather | bytes 778240 | tf_op jit(solution)/shard_map/all_gather | solution.py:310
  497.0 8.6 %all-gather.4 = bf16[160,2432]{1,0:T(8,128)(2,1)S(1)} all-gather(bf16[40,2432]{1,0:T(8,128)(2,1)S(1)} %get-tuple-element.59), channel_id=6, replica_groups=mesh['rep'=4,'shard'=8] {'rep'}, dimensions={0}, use_global_device_ids=true | all-gather | bytes 972800 | tf_op jit(solution)/shard_map/all_gather | solution.py:310
  505.7 7.8 %all-gather.6 = bf16[128,2432]{1,0:T(8,128)(2,1)S(1)} all-gather(bf16[32,2432]{1,0:T(8,128)(2,1)S(1)} %get-tuple-element.58), channel_id=8, replica_groups=mesh['rep'=4,'shard'=8] {'rep'}, dimensions={0}, use_global_device_ids=true | all-gather | bytes 778240 | tf_op jit(solution)/shard_map/all_gather | solution.py:310
  513.5 8.9 %all-gather.5 = bf16[160,2432]{1,0:T(8,128)(2,1)S(1)} all-gather(bf16[40,2432]{1,0:T(8,128)(2,1)S(1)} %get-tuple-element.60), channel_id=7, replica_groups=mesh['rep'=4,'shard'=8] {'rep'}, dimensions={0}, use_global_device_ids=true | all-gather | bytes 972800 | tf_op jit(solution)/shard_map/all_gather | solution.py:310
  522.7 1.2 fusion.58
  523.8 1.1 fusion.59
  525.0 1.1 fusion.60
  526.1 1.2 fusion.61
  527.3 2.9 concatenate.126
  530.3 1.5 convert_element_type.177
  531.7 3.6 concatenate.125
  535.3 1.5 convert_element_type.176
  537.0 1.5 copy.118
  (179 shorter events, 30.3 us)
Async XLA Ops:
  7.2 127.0 %all-gather.12.cloned.1.call-start = ((), (), s32[]{:S(2)}) async-start(), calls=%async_computation.4 | async-start | bytes 4386816 | tf_op jit(solution)/shard_map/all_gather | solution.py:183
  12.2 0.8 copy-start.3
  12.2 4.1 copy-start.30
  13.0 173.9 %all-gather.14.cloned.1.call-start = ((), (), s32[]{:S(2)}) async-start(), calls=%async_computation.5 | async-start | bytes 4902912 | tf_op jit(solution)/shard_map/all_gather | solution.py:194
  13.1 5.4 copy-start
  16.2 213.0 %reduce-scatter.7.cloned.1.call-start = ((), (), s32[]{:S(2)}) async-start(), calls=%async_computation.6 | async-start | bytes 2293760 | tf_op jit(solution)/shard_map/reduce_scatter | solution.py:235
  122.3 2.3 copy-start.4
  124.4 14.9 %copy-start.27 = (f32[128]{0:T(128)}, f32[128]{0:T(128)S(1)}, u32[]{:S(2)}) copy-start(f32[128]{0:T(128)S(1)} %get-tuple-element.147) | copy-start | bytes 1540
  124.6 15.2 %copy-start.10 = (f32[128,32]{0,1:T(8,128)}, f32[128,32]{0,1:T(8,128)S(1)}, u32[]{:S(2)}) copy-start(f32[128,32]{0,1:T(8,128)S(1)} %get-tuple-element.144) | copy-start | bytes 49156
  124.6 15.2 %copy-start.12 = (f32[128,32]{0,1:T(8,128)}, f32[128,32]{0,1:T(8,128)S(1)}, u32[]{:S(2)}) copy-start(f32[128,32]{0,1:T(8,128)S(1)} %get-tuple-element.145) | copy-start | bytes 49156
  134.2 58.3 %copy-start.5 = (bf16[512,896]{1,0:T(8,128)(2,1)}, bf16[512,896]{1,0:T(8,128)(2,1)S(1)}, u32[]{:S(2)}) copy-start(bf16[512,896]{1,0:T(8,128)(2,1)S(1)} %all_gather.73) | copy-start | bytes 2752516
  137.1 2.2 copy-start.23
  139.4 1.4 copy-start.14
  139.8 0.7 copy-start.19
  139.8 0.7 copy-start.21
  139.9 0.6 copy-start.8
  140.2 3.4 copy-start.18
  140.5 0.6 copy-start.16
  143.6 86.6 %copy-start.26 = (f32[128]{0:T(128)}, f32[128]{0:T(128)S(1)}, u32[]{:S(2)}) copy-start(f32[128]{0:T(128)S(1)} %get-tuple-element.149) | copy-start | bytes 1540
  186.9 5.5 %copy-start.2 = (bf16[8,152,896]{2,1,0:T(8,128)(2,1)S(1)}, bf16[8,152,896]{2,1,0:T(8,128)(2,1)}, u32[]{:S(2)}) copy-start(bf16[8,152,896]{2,1,0:T(8,128)(2,1)} %pad_maximum_fusion.3) | copy-start | bytes 6537220
  186.9 9.7 %slice-start = ((s8[4358144]{0:T(1024)(128)(4,1)}), s8[4194304]{0:T(1024)(128)(4,1)S(1)}, s32[]{:S(2)}) async-start(s8[4358144]{0:T(1024)(128)(4,1)} %bitcast.198), calls=%async_computation.10 | async-start | bytes 8388608
  192.5 4.2 slice-start.1
  195.0 1.6 copy-start.31
  195.0 4.5 copy-start.33
  195.0 4.5 copy-start.35
  201.0 127.6 %reduce-scatter.9.cloned.1.call-start = ((), (), s32[]{:S(2)}) async-start(), calls=%async_computation.7 | async-start | bytes 4386816 | tf_op jit(solution)/shard_map/reduce_scatter | solution.py:291
  232.5 2.3 copy-start.17
  232.5 2.7 copy-start.15
  234.6 1.0 copy-start.9
  234.6 1.3 copy-start.20
  234.6 1.3 copy-start.22
  234.9 1.3 copy-start.11
  234.9 1.3 copy-start.13
  236.2 2.1 copy-start.24
  236.2 2.1 copy-start.28
  236.6 2.6 copy-start.25
  236.6 2.7 copy-start.1
  244.1 88.1 %copy-start.6 = (bf16[512,896]{1,0:T(8,128)(2,1)S(1)}, bf16[512,896]{1,0:T(8,128)(2,1)}, u32[]{:S(2)}) copy-start(bf16[512,896]{1,0:T(8,128)(2,1)} %copy-done.5) | copy-start | bytes 2752516
  244.1 88.1 %copy-start.32 = (bf16[512,1216]{0,1:T(8,128)(2,1)S(1)}, bf16[512,1216]{0,1:T(8,128)(2,1)}, u32[]{:S(2)}) copy-start(bf16[512,1216]{0,1:T(8,128)(2,1)} %copy-done.31) | copy-start | bytes 3735556
  244.1 109.8 %reduce-scatter.11.cloned.1.call-start = ((), (), s32[]{:S(2)}) async-start(), calls=%async_computation.8 | async-start | bytes 716800 | tf_op jit(solution)/shard_map/reduce_scatter | solution.py:298
  332.2 147.2 %reduce-scatter.13.cloned.1.call-start = ((), (), s32[]{:S(2)}) async-start(), calls=%async_computation.9 | async-start | bytes 7354368
  333.7 1.2 copy-start.7
  333.7 1.6 copy-start.34
  333.7 1.9 copy-start.36
  345.8 0.7 copy-start.29
Sparse Core Ops, SparseCore 0:
  13.1 96.6 all-gather.11
  112.6 74.2 all-gather.13
  201.1 28.0 reduce-scatter.6
  244.2 84.2 reduce-scatter.8
  332.3 21.5 reduce-scatter.10
  357.4 121.9 reduce-scatter.12
